TPU v7x, 32 devices: a whole 2x2x4 slice. The times are simulated.
32 devices in a mesh: pipe: 2 (over y), tensor: 4 (over z), dp: 4 (over x, core).
Axes of the slice: x: 2, y: 2, z: 4, core: 2. Of those that a mesh axis runs over, the one named last changes fastest.
Arguments:
- weights: bfloat16 [2, 4096, 4096], P('pipe', None, 'tensor'), may hold values from -0.09375 to 0.09375
- codes: int32 [2, 1024, 4096], P('pipe', 'dp'), may hold values from -127 to 127
- scales: float32 [2, 1024], P('pipe', 'dp'), may hold values from 0.004 to 0.04
- grad_out: bfloat16 [1024, 4096], P('dp', 'tensor'), may hold values from -6 to 6
Outputs:
- grad_in: bfloat16 [2, 1024, 4096], P('pipe', 'dp', 'tensor')
- weight_grad: float32 [2, 4096, 4096], P('pipe', 'dp', 'tensor')
Inputs may be any that keep to these rules, and one draw needn't show every extreme that they name: Symmetric integer codes of a per-token quantization.
All inputs are finite; a program needn't handle non-finite values.
Results may differ from a plain program's by a relative error of at most 0.028.
Values may be sent and summed in bfloat16 or wider, within the bound.
A program may use at most 64 MiB of HBM per device.

v0:
```python
import jax
import jax.numpy as jnp
from jax import lax
from jax.sharding import PartitionSpec as P

MICRO = 4


def shifted(value, axis, steps):
    count = lax.axis_size(axis)
    initial, last = (max(0, -steps), min(count, count - steps))
    return lax.ppermute(value, axis, [(source, source + steps) for source in range(initial, last)])


def per_device(weights, codes, scales, grad_out):
    section_count = lax.axis_size("pipe")
    section_index = lax.axis_index("pipe")
    w_local = weights[0]
    tok_rows = codes.shape[1]
    micro_rows = tok_rows // MICRO
    col_count = w_local.shape[1]
    incoming = jnp.zeros((micro_rows, col_count), jnp.bfloat16)
    arrived_all = jnp.zeros((tok_rows, col_count), jnp.bfloat16)
    leaving_all = jnp.zeros((tok_rows, col_count), jnp.bfloat16)
    slot_count = MICRO + section_count - 1
    for step_index in range(slot_count):
        micro_index = step_index - (section_count - 1 - section_index)
        is_valid = (micro_index >= 0) & (micro_index < MICRO)
        row_start = jnp.clip(micro_index, 0, MICRO - 1) * micro_rows
        seed_rows = lax.dynamic_slice_in_dim(grad_out, row_start, micro_rows, 0)
        arriving = jnp.where(section_index == section_count - 1, seed_rows, incoming)
        partial_value = lax.dot_general(
            arriving, w_local, (((1,), (1,)), ((), ())), preferred_element_type=jnp.float32
        )
        summed = lax.psum_scatter(
            partial_value.astype(jnp.bfloat16), "tensor", scatter_dimension=1, tiled=True
        ).astype(jnp.float32)
        result = (arriving.astype(jnp.float32) + summed).astype(jnp.bfloat16)
        arrived_all = jnp.where(
            is_valid,
            lax.dynamic_update_slice_in_dim(arrived_all, arriving, row_start, 0),
            arrived_all,
        )
        leaving_all = jnp.where(
            is_valid,
            lax.dynamic_update_slice_in_dim(leaving_all, result, row_start, 0),
            leaving_all,
        )
        if step_index + 1 < slot_count:
            incoming = shifted(result, "pipe", -1)
    dequant = (codes[0].astype(jnp.float32) * scales[0][:, None]).astype(jnp.bfloat16)
    spread = lax.all_to_all(dequant, "dp", split_axis=1, concat_axis=0, tiled=True)
    shard_rows = lax.all_gather(arrived_all, "dp", axis=0, tiled=True)
    piece_rows = shard_rows.shape[0]
    group_count = piece_rows // tok_rows
    x_groups = spread.reshape(group_count, tok_rows, spread.shape[1])
    g_groups = shard_rows.reshape(group_count, tok_rows, shard_rows.shape[1])
    group_terms = jnp.einsum(
        "ntk,ntc->nkc", x_groups, g_groups, preferred_element_type=jnp.float32
    ).astype(jnp.bfloat16)
    grad_weight = jnp.sum(group_terms.astype(jnp.float32), axis=0)
    return (leaving_all[None], grad_weight[None])


def solution(mesh):
    placed = (P("pipe", None, "tensor"), P("pipe", "dp", None), P("pipe", "dp"), P("dp", "tensor"))
    return jax.shard_map(
        per_device,
        mesh=mesh,
        in_specs=placed,
        out_specs=(P("pipe", "dp", "tensor"), P("pipe", "dp", "tensor")),
        check_vma=False,
    )
```

profile of v0, /device:TPU:0, one launch (start us, length us, event | category | flops | bytes accessed | tf_op | source)
XLA Modules:
  0.0 224.5 jit_solution(11132003625899314082)
XLA Ops:
  7.2 0.0 reduce-scatter.6.cloned.1.call-start
  7.2 7.0 %fusion.10 = bf16[64,4096]{1,0:T(8,128)(2,1)} fusion(bf16[1,4096,1024]{2,1,0:T(8,128)(2,1)} %param.4, bf16[256,1024]{1,0:T(8,128)(2,1)} %param.7, s32[]{:T(128)S(6)} %select_n.139, pred[]{:T(512)S(6)} %eq.2), kind=kOutput, calls=%fused_computation.11 | convolution fusion | flops 537198592 | bytes 9043973 | tf_op jit(solution)/shard_map/dot_general | solution.py:32
  14.2 0.0 reduce-scatter.6.cloned.1.call-update
  14.2 0.0 reduce-scatter.8.cloned.1.call-start
  14.3 24.7 %reduce-scatter.6.cloned.1.call-done = bf16[64,1024]{1,0:T(8,128)(2,1)} async-done(((bf16[64,4096]{1,0:T(8,128)(2,1)}), bf16[64,1024]{1,0:T(8,128)(2,1)}) %reduce-scatter.6.cloned.1.call-update) | async-done | bytes 131088 | tf_op jit(solution)/shard_map/reduce_scatter | solution.py:35
  39.0 0.1 broadcast.25.clone
  39.0 1.0 select_dynamic-update-slice_fusion.8
  40.0 1.3 collective-permute-start
  41.3 0.1 broadcast.25.clone.1
  41.4 5.5 %collective-permute-done = bf16[64,1024]{1,0:T(8,128)(2,1)S(1)} collective-permute-done((bf16[64,1024]{1,0:T(8,128)(2,1)S(1)}, bf16[64,1024]{1,0:T(8,128)(2,1)S(1)}, u32[]{:S(2)}, u32[]{:S(2)}) %collective-permute-start) | collective-permute-done | bytes 131104 | tf_op jit(solution)/shard_map/ppermute | solution.py:12
  46.9 0.1 select_dynamic-update-slice_fusion.3
  46.9 6.8 %fusion.13 = bf16[64,4096]{1,0:T(8,128)(2,1)} fusion(bf16[64,1024]{1,0:T(8,128)(2,1)S(1)} %get-tuple-element.9, bf16[1,4096,1024]{2,1,0:T(8,128)(2,1)} %param.4), kind=kOutput, calls=%fused_computation.12 | convolution fusion | flops 537133056 | bytes 9043968 | tf_op jit(solution)/shard_map/dot_general | solution.py:32
  53.8 0.0 reduce-scatter.8.cloned.1.call-update
  53.8 0.0 reduce-scatter.10.cloned.1.call-start
  53.8 19.2 %reduce-scatter.8.cloned.1.call-done = bf16[64,1024]{1,0:T(8,128)(2,1)} async-done(((bf16[64,4096]{1,0:T(8,128)(2,1)}), bf16[64,1024]{1,0:T(8,128)(2,1)}) %reduce-scatter.8.cloned.1.call-update) | async-done | bytes 131088 | tf_op jit(solution)/shard_map/reduce_scatter | solution.py:35
  73.1 1.0 select_dynamic-update-slice_fusion.7
  74.0 1.3 collective-permute-start.1
  75.3 5.6 %collective-permute-done.1 = bf16[64,1024]{1,0:T(8,128)(2,1)S(1)} collective-permute-done((bf16[64,1024]{1,0:T(8,128)(2,1)S(1)}, bf16[64,1024]{1,0:T(8,128)(2,1)S(1)}, u32[]{:S(2)}, u32[]{:S(2)}) %collective-permute-start.1) | collective-permute-done | bytes 131104 | tf_op jit(solution)/shard_map/ppermute | solution.py:12
  80.9 0.1 select_dynamic-update-slice_fusion.2
  81.0 6.8 %fusion.16 = bf16[64,4096]{1,0:T(8,128)(2,1)} fusion(bf16[64,1024]{1,0:T(8,128)(2,1)S(1)} %get-tuple-element.7, bf16[1,4096,1024]{2,1,0:T(8,128)(2,1)} %param.4), kind=kOutput, calls=%fused_computation.13 | convolution fusion | flops 537133056 | bytes 9043968 | tf_op jit(solution)/shard_map/dot_general | solution.py:32
  87.8 0.0 reduce-scatter.10.cloned.1.call-update
  87.8 0.0 reduce-scatter.12.cloned.1.call-start
  87.9 19.3 %reduce-scatter.10.cloned.1.call-done = bf16[64,1024]{1,0:T(8,128)(2,1)} async-done(((bf16[64,4096]{1,0:T(8,128)(2,1)}), bf16[64,1024]{1,0:T(8,128)(2,1)}) %reduce-scatter.10.cloned.1.call-update) | async-done | bytes 131088 | tf_op jit(solution)/shard_map/reduce_scatter | solution.py:35
  107.2 1.0 select_dynamic-update-slice_fusion.6
  108.1 1.3 collective-permute-start.2
  109.4 5.6 %collective-permute-done.2 = bf16[64,1024]{1,0:T(8,128)(2,1)S(1)} collective-permute-done((bf16[64,1024]{1,0:T(8,128)(2,1)S(1)}, bf16[64,1024]{1,0:T(8,128)(2,1)S(1)}, u32[]{:S(2)}, u32[]{:S(2)}) %collective-permute-start.2) | collective-permute-done | bytes 131104 | tf_op jit(solution)/shard_map/ppermute | solution.py:12
  115.0 0.1 select_dynamic-update-slice_fusion.1
  115.1 6.8 %fusion.19 = bf16[64,4096]{1,0:T(8,128)(2,1)} fusion(bf16[64,1024]{1,0:T(8,128)(2,1)S(1)} %get-tuple-element.5, bf16[1,4096,1024]{2,1,0:T(8,128)(2,1)} %param.4), kind=kOutput, calls=%fused_computation.14 | convolution fusion | flops 537133056 | bytes 9043968 | tf_op jit(solution)/shard_map/dot_general | solution.py:32
  121.9 0.0 reduce-scatter.12.cloned.1.call-update
  121.9 0.0 reduce-scatter.14.cloned.1.call-start
  122.0 19.3 %reduce-scatter.12.cloned.1.call-done = bf16[64,1024]{1,0:T(8,128)(2,1)} async-done(((bf16[64,4096]{1,0:T(8,128)(2,1)}), bf16[64,1024]{1,0:T(8,128)(2,1)}) %reduce-scatter.12.cloned.1.call-update) | async-done | bytes 131088 | tf_op jit(solution)/shard_map/reduce_scatter | solution.py:35
  141.2 1.0 select_dynamic-update-slice_fusion.5
  142.2 1.3 collective-permute-start.3
  143.5 5.6 %collective-permute-done.3 = bf16[64,1024]{1,0:T(8,128)(2,1)S(1)} collective-permute-done((bf16[64,1024]{1,0:T(8,128)(2,1)S(1)}, bf16[64,1024]{1,0:T(8,128)(2,1)S(1)}, u32[]{:S(2)}, u32[]{:S(2)}) %collective-permute-start.3) | collective-permute-done | bytes 131104 | tf_op jit(solution)/shard_map/ppermute | solution.py:12
  149.1 0.1 select_dynamic-update-slice_fusion
  149.2 7.0 %fusion.22 = bf16[64,4096]{1,0:T(8,128)(2,1)} fusion(bf16[64,1024]{1,0:T(8,128)(2,1)S(1)} %get-tuple-element.3, bf16[1,4096,1024]{2,1,0:T(8,128)(2,1)} %param.4), kind=kOutput, calls=%fused_computation.15 | convolution fusion | flops 537133056 | bytes 9043968 | tf_op jit(solution)/shard_map/dot_general | solution.py:32
  156.2 0.0 reduce-scatter.14.cloned.1.call-update
  156.2 0.2 all-gather.2.cloned.1.call-start
  156.4 0.3 all-gather.2.cloned.1.call-update
  156.8 0.0 copy-start.3
  156.8 4.6 %convert_element_type.97 = f32[1,256,4096]{2,1,0:T(8,128)} convert(s32[1,256,4096]{2,1,0:T(8,128)} %param.5) | non-fusion elementwise | flops 1048576 | bytes 8388608 | tf_op jit(solution)/shard_map/convert_element_type | solution.py:51
  161.4 5.6 %copy.6 = f32[1,256,4096]{1,2,0:T(8,128)} copy(f32[1,256,4096]{2,1,0:T(8,128)} %convert_element_type.97) | data formatting | bytes 8388608 | tf_op jit(solution)/shard_map/convert_element_type | solution.py:51
  167.1 3.9 %multiply_convert_fusion = bf16[256,4,1024]{0,2,1:T(8,128)(2,1)} fusion(f32[256,4,1024]{0,2,1:T(8,128)} %bitcast.38, f32[256]{0:T(256)S(1)} %bitcast.40), kind=kLoop, calls=%fused_computation.16 | loop fusion | flops 2097152 | bytes 6292480 | tf_op jit(solution)/shard_map/convert_element_type | solution.py:51
  170.9 3.6 %all-to-all-start = ((bf16[256,4,1024]{0,2,1:T(8,128)(2,1)}), bf16[256,4,1024]{0,2,1:T(8,128)(2,1)S(1)}, u32[]{:S(2)}, u32[]{:S(2)}) async-start(bf16[256,4,1024]{0,2,1:T(8,128)(2,1)} %multiply_convert_fusion), calls=%async_computation.5 | async-start | bytes 4194304 | tf_op jit(solution)/shard_map/all_to_all | solution.py:52
  174.6 0.9 reduce-scatter.14.cloned.1.call-done
  175.5 1.0 fusion.28
  176.5 35.0 %all-to-all-done = bf16[256,4,1024]{0,2,1:T(8,128)(2,1)S(1)} async-done(((bf16[256,4,1024]{0,2,1:T(8,128)(2,1)}), bf16[256,4,1024]{0,2,1:T(8,128)(2,1)S(1)}, u32[]{:S(2)}, u32[]{:S(2)}) %all-to-all-start) | async-done | bytes 2097184 | tf_op jit(solution)/shard_map/all_to_all | solution.py:52
  211.4 6.2 %convert_reduce_fusion = f32[1024,1024]{1,0:T(8,128)} fusion(bf16[4,256,1024]{2,1,0:T(8,128)(2,1)} %bitcast.41, bf16[256,4,1024]{0,2,1:T(8,128)(2,1)S(1)} %all-to-all-done), kind=kOutput, calls=%fused_computation | convolution fusion | flops 2159017984 | bytes 8388608 | tf_op jit(solution)/shard_map/ntk,ntc->nkc/dot_general | solution.py:58
  (10 shorter events, 0.1 us)
Async XLA Ops:
  7.2 31.9 %copy-start.1 = (bf16[256,1024]{1,0:T(8,128)(2,1)S(1)}, bf16[256,1024]{1,0:T(8,128)(2,1)}, u32[]{:S(2)}) copy-start(bf16[256,1024]{1,0:T(8,128)(2,1)} %param.7) | copy-start | bytes 1572868
  7.2 31.8 %reduce-scatter.6.cloned.1.call-start = ((), (), s32[]{:S(2)}) async-start(), calls=%async_computation.6 | async-start | bytes 655360 | tf_op jit(solution)/shard_map/reduce_scatter | solution.py:35
  14.2 58.9 %reduce-scatter.8.cloned.1.call-start = ((), (), s32[]{:S(2)}) async-start(), calls=%async_computation.7 | async-start | bytes 655360 | tf_op jit(solution)/shard_map/reduce_scatter | solution.py:35
  40.0 6.9 %collective-permute-start = (bf16[64,1024]{1,0:T(8,128)(2,1)S(1)}, bf16[64,1024]{1,0:T(8,128)(2,1)S(1)}, u32[]{:S(2)}, u32[]{:S(2)}) collective-permute-start(bf16[64,1024]{1,0:T(8,128)(2,1)S(1)} %get-tuple-element.17), channel_id=1, source_target_pairs={{16,0},{17,1},{18,2},{19,3},{20,4},{21,5},{22,6},{23,7},{24,8},{25... | collective-permute-start | bytes 393224 | tf_op jit(solution)/shard_map/ppermute | solution.py:12
  53.8 53.4 %reduce-scatter.10.cloned.1.call-start = ((), (), s32[]{:S(2)}) async-start(), calls=%async_computation.8 | async-start | bytes 655360 | tf_op jit(solution)/shard_map/reduce_scatter | solution.py:35
  74.0 6.9 %collective-permute-start.1 = (bf16[64,1024]{1,0:T(8,128)(2,1)S(1)}, bf16[64,1024]{1,0:T(8,128)(2,1)S(1)}, u32[]{:S(2)}, u32[]{:S(2)}) collective-permute-start(bf16[64,1024]{1,0:T(8,128)(2,1)S(1)} %get-tuple-element.15), channel_id=1, source_target_pairs={{16,0},{17,1},{18,2},{19,3},{20,4},{21,5},{22,6},{23,7},{24,8},{25... | collective-permute-start | bytes 393224 | tf_op jit(solution)/shard_map/ppermute | solution.py:12
  87.8 53.4 %reduce-scatter.12.cloned.1.call-start = ((), (), s32[]{:S(2)}) async-start(), calls=%async_computation.9 | async-start | bytes 655360 | tf_op jit(solution)/shard_map/reduce_scatter | solution.py:35
  108.1 6.9 %collective-permute-start.2 = (bf16[64,1024]{1,0:T(8,128)(2,1)S(1)}, bf16[64,1024]{1,0:T(8,128)(2,1)S(1)}, u32[]{:S(2)}, u32[]{:S(2)}) collective-permute-start(bf16[64,1024]{1,0:T(8,128)(2,1)S(1)} %get-tuple-element.13), channel_id=1, source_target_pairs={{16,0},{17,1},{18,2},{19,3},{20,4},{21,5},{22,6},{23,7},{24,8},{25... | collective-permute-start | bytes 393224 | tf_op jit(solution)/shard_map/ppermute | solution.py:12
  121.9 53.6 %reduce-scatter.14.cloned.1.call-start = ((), (), s32[]{:S(2)}) async-start(), calls=%async_computation.10 | async-start | bytes 655360 | tf_op jit(solution)/shard_map/reduce_scatter | solution.py:35
  142.2 6.9 %collective-permute-start.3 = (bf16[64,1024]{1,0:T(8,128)(2,1)S(1)}, bf16[64,1024]{1,0:T(8,128)(2,1)S(1)}, u32[]{:S(2)}, u32[]{:S(2)}) collective-permute-start(bf16[64,1024]{1,0:T(8,128)(2,1)S(1)} %get-tuple-element.11), channel_id=1, source_target_pairs={{16,0},{17,1},{18,2},{19,3},{20,4},{21,5},{22,6},{23,7},{24,8},{25... | collective-permute-start | bytes 393224 | tf_op jit(solution)/shard_map/ppermute | solution.py:12
  149.1 7.3 %copy-start = (bf16[256,1024]{1,0:T(8,128)(2,1)}, bf16[256,1024]{1,0:T(8,128)(2,1)S(1)}, u32[]{:S(2)}) copy-start(bf16[256,1024]{1,0:T(8,128)(2,1)S(1)} %get-tuple-element.2) | copy-start | bytes 1572868
  156.2 55.2 %all-gather.2.cloned.1.call-start = ((), (), s32[]{:S(2)}) async-start(), calls=%async_computation.11 | async-start | bytes 2621440 | tf_op jit(solution)/shard_map/all_gather | solution.py:53
  156.8 10.3 %copy-start.3 = (f32[1,256]{1,0:T(1,128)S(1)}, f32[1,256]{1,0:T(1,128)}, u32[]{:S(2)}) copy-start(f32[1,256]{1,0:T(1,128)} %param.6) | copy-start | bytes 3076
  170.9 40.5 %all-to-all-start = ((bf16[256,4,1024]{0,2,1:T(8,128)(2,1)}), bf16[256,4,1024]{0,2,1:T(8,128)(2,1)S(1)}, u32[]{:S(2)}, u32[]{:S(2)}) async-start(bf16[256,4,1024]{0,2,1:T(8,128)(2,1)} %multiply_convert_fusion), calls=%async_computation.5 | async-start | bytes 4194304 | tf_op jit(solution)/shard_map/all_to_all | solution.py:52
  176.5 41.2 %copy-start.2 = (bf16[1,256,1024]{2,1,0:T(8,128)(2,1)}, bf16[1,256,1024]{2,1,0:T(8,128)(2,1)S(1)}, u32[]{:S(2)}) copy-start(bf16[1,256,1024]{2,1,0:T(8,128)(2,1)S(1)} %fusion.28) | copy-start | bytes 1572868
Sparse Core Ops, SparseCore 0:
  14.3 24.5 reduce-scatter.5
  53.9 19.1 reduce-scatter.7
  88.0 19.1 reduce-scatter.9
  122.1 19.1 reduce-scatter.11
  156.3 19.1 reduce-scatter.13
  176.9 32.0 all-gather.1
where the time goes:
time: 225 us
  waiting for transfers between devices  141 us (63%)
  matrix products  40.7 us (18%)
  between operations  14.3 us (6%)
  other arithmetic  13.6 us (6%)
  starting transfers between devices  9.21 us (4%)
  local copies, waits for them, and re-layouts  5.78 us (3%)
    reduce_scatter x5, waiting for transfers between devices, per_device(): lax.psum_scatter(partial_value.astype(jnp.bfloat16), 'tensor', scatter_di...  83.4 us
    all_to_all x1, waiting for transfers between devices, per_device(): lax.all_to_all(dequant, 'dp', split_axis=1, concat_axis=0, tiled=True)  35 us
    dot_general x5, matrix products, per_device(): lax.dot_general(arriving, w_local, (((1,), (1,)), ((), ())), preferred_el...  34.5 us
    ppermute x4, waiting for transfers between devices, shifted(): lax.ppermute(value, axis, [(source, source + steps) for source in range(i...  22.1 us
    dot_general x1, matrix products, per_device(): jnp.einsum('ntk,ntc->nkc', x_groups, g_groups, preferred_element_type=jnp...  6.22 us
    convert_element_type x1, local copies, waits for them, and re-layouts, per_device(): codes[0].astype(jnp.float32) * scales[0][:, None]  5.62 us
    ppermute x4, starting transfers between devices, shifted(): lax.ppermute(value, axis, [(source, source + steps) for source in range(i...  5.17 us
    select_n x5, other arithmetic, per_device(): jnp.where(is_valid, lax.dynamic_update_slice_in_dim(leaving_all, result,...  4.8 us
  transfers between devices with their start and end apart: 11, of which 10 were waited for; matrix products, arithmetic and copies ran while one was open for 7% of the time, Pallas kernels for 0%

commit v1 on v0

v1 whole, which is shorter than its diff:
```python
import functools

import jax
import jax.numpy as jnp
from jax import lax
from jax.experimental import pallas as pl
from jax.experimental.pallas import tpu as pltpu
from jax.sharding import PartitionSpec as P

MICRO = 4
NT = (((1,), (1,)), ((), ()))


def relay_kernel(
    weights, codes, scales, grad_out,
    grad_in, g_all, x_all,
    w_buf, c_buf, x_buf, g_buf, prod, from_left, from_right,
    w_sem, c_sem, g_sem, hop_sem,
    right_send, right_recv, left_send, left_recv,
    g_send, g_recv, x_send, x_recv, g_own, x_own,
    *, sections, shards, replicas, micro,
):
    section, shard, replica = (lax.axis_index(n) for n in ("pipe", "tensor", "dp"))
    is_last = section == sections - 1
    tok, cols = g_buf.shape
    rows = tok // micro
    width = x_buf.shape[2]

    barrier = pltpu.get_barrier_semaphore()

    def greet(condition, target):
        @pl.when(condition)
        def _():
            pl.semaphore_signal(barrier, inc=1, device_id=target)

    def w_copy(j):
        part = pl.ds(pl.multiple_of(j * cols, cols), cols)
        return pltpu.make_async_copy(weights.at[part, :], w_buf.at[part, :], w_sem.at[j])

    def c_copy(o):
        peer = lax.rem(replica + o, replicas)
        part = pl.ds(pl.multiple_of(peer * width, width), width)
        return pltpu.make_async_copy(codes.at[:, part], c_buf.at[o], c_sem.at[o])

    def micro_rows(m):
        return pl.ds(pl.multiple_of(m * rows, rows), rows)

    def g_load(m):
        return pltpu.make_async_copy(grad_out.at[micro_rows(m), :], g_buf.at[micro_rows(m), :], g_sem.at[m])

    def order(i):
        return jnp.where(2 * shard < shards, shards - 1 - i, i)

    @pl.when(is_last)
    def _():
        @pl.loop(0, micro)
        def _(m):
            g_load(m).start()

    @pl.loop(0, shards)
    def _(i):
        w_copy(order(i)).start()

    @pl.loop(0, replicas)
    def _(o):
        c_copy(o).start()

    greet(shard > 0, {"tensor": shard - 1})
    greet(shard < shards - 1, {"tensor": shard + 1})
    greet(section > 0, {"pipe": section - 1})
    greet(section < sections - 1, {"pipe": section + 1})

    @pl.loop(1, replicas)
    def _(o):
        pl.semaphore_signal(barrier, inc=1, device_id={"dp": lax.rem(replica + o, replicas)})

    def one(condition):
        return jnp.where(condition, 1, 0)

    pl.semaphore_wait(
        barrier,
        replicas - 1 + one(shard > 0) + one(shard < shards - 1) + one(section > 0) + one(section < sections - 1),
    )

    def hop(m):
        return pltpu.make_async_remote_copy(
            src_ref=grad_in.at[micro_rows(m), :], dst_ref=g_buf.at[micro_rows(m), :],
            send_sem=hop_sem.at[m], recv_sem=g_sem.at[m], device_id={"pipe": section - 1})

    def to_right(m, j):
        return pltpu.make_async_remote_copy(
            src_ref=prod.at[m, j], dst_ref=from_left.at[m, j],
            send_sem=right_send.at[m, j], recv_sem=right_recv.at[m, j], device_id={"tensor": shard + 1})

    def to_left(m, j):
        return pltpu.make_async_remote_copy(
            src_ref=prod.at[m, j], dst_ref=from_right.at[m, j],
            send_sem=left_send.at[m, j], recv_sem=left_recv.at[m, j], device_id={"tensor": shard - 1})

    def own_rows(source):
        return pl.ds(pl.multiple_of(source * tok, tok), tok)

    def g_share(m, o):
        landing = pl.ds(pl.multiple_of(replica * tok + m * rows, rows), rows)
        return pltpu.make_async_remote_copy(
            src_ref=g_buf.at[micro_rows(m), :], dst_ref=g_all.at[landing, :],
            send_sem=g_send.at[m, o], recv_sem=g_recv.at[m, o],
            device_id={"dp": lax.rem(replica + o, replicas)})

    def g_keep(m):
        landing = pl.ds(pl.multiple_of(replica * tok + m * rows, rows), rows)
        return pltpu.make_async_copy(g_buf.at[micro_rows(m), :], g_all.at[landing, :], g_own.at[m])

    def x_share(o):
        return pltpu.make_async_remote_copy(
            src_ref=x_buf.at[o], dst_ref=x_all.at[own_rows(replica), :],
            send_sem=x_send.at[o], recv_sem=x_recv.at[o],
            device_id={"dp": lax.rem(replica + o, replicas)})

    def x_keep():
        return pltpu.make_async_copy(x_buf.at[0], x_all.at[own_rows(replica), :], x_own)

    def dequantize():
        @pl.loop(0, replicas)
        def _(i):
            o = replicas - 1 - i
            c_copy(o).wait()

            @pl.loop(0, micro)
            def _(m):
                part = micro_rows(m)
                value = c_buf[o, part, :].astype(jnp.float32) * scales[part, :]
                x_buf[o, part, :] = value.astype(jnp.bfloat16)

            @pl.when(o > 0)
            def _():
                x_share(o).start()

        x_keep().start()

    def produce(m):
        @pl.when(is_last)
        def _():
            g_load(m).wait()

        @pl.when(jnp.logical_not(is_last))
        def _():
            hop(m).wait_recv()

        @pl.loop(0, shards)
        def _(i):
            j = order(i)

            @pl.when(m == 0)
            def _():
                w_copy(j).wait()

            part = pl.ds(pl.multiple_of(j * cols, cols), cols)
            prod[m, j] = lax.dot_general(
                g_buf[micro_rows(m), :], w_buf[part, :], NT, preferred_element_type=jnp.float32
            ).astype(jnp.bfloat16)

            @pl.when((shard == 0) & (j > 0))
            def _():
                to_right(m, j).start()

            @pl.when((shard == shards - 1) & (j < shards - 1))
            def _():
                to_left(m, j).start()

        g_keep(m).start()

        @pl.loop(1, replicas)
        def _(o):
            g_share(m, o).start()

    def add_in(m, j, arrived):
        total = prod[m, j].astype(jnp.float32) + arrived[m, j].astype(jnp.float32)
        prod[m, j] = total.astype(jnp.bfloat16)

    def relay(m):
        @pl.loop(0, shards - 1)
        def _(i):
            far = shards - 1 - i

            @pl.when((shard > 0) & (shard + far < shards))
            def _():
                j = shard + far
                to_right(m, j).wait_recv()
                add_in(m, j, from_left)
                to_right(m, j).start()

            @pl.when((shard < shards - 1) & (shard - far >= 0))
            def _():
                j = shard - far
                to_left(m, j).wait_recv()
                add_in(m, j, from_right)
                to_left(m, j).start()

    def finish(m):
        part = micro_rows(m)

        @pl.when(shard > 0)
        def _():
            to_right(m, shard).wait_recv()

        @pl.when(shard < shards - 1)
        def _():
            to_left(m, shard).wait_recv()

        own = prod[m, shard].astype(jnp.float32) + g_buf[part, :].astype(jnp.float32)

        @pl.when((shard > 0) & (shard < shards - 1))
        def _():
            both = from_left[m, shard].astype(jnp.float32) + from_right[m, shard].astype(jnp.float32)
            grad_in[part, :] = (own + both).astype(jnp.bfloat16)

        @pl.when(shard == 0)
        def _():
            grad_in[part, :] = (own + from_right[m, shard].astype(jnp.float32)).astype(jnp.bfloat16)

        @pl.when(shard == shards - 1)
        def _():
            grad_in[part, :] = (own + from_left[m, shard].astype(jnp.float32)).astype(jnp.bfloat16)

        @pl.when(section > 0)
        def _():
            hop(m).start()

    @pl.when(jnp.logical_not(is_last))
    def _():
        dequantize()

    @pl.loop(0, micro + 1)
    def _(i):
        @pl.when(i < micro)
        def _():
            produce(i)

        @pl.when((i == 0) & is_last)
        def _():
            dequantize()

        @pl.when(i > 0)
        def _():
            finish(i - 1)

        @pl.when(i < micro)
        def _():
            relay(i)

    @pl.loop(0, micro)
    def _(m):
        @pl.loop(0, shards)
        def _(j):
            @pl.when((j > shard))
            def _():
                to_right(m, j).wait_send()

            @pl.when((j < shard))
            def _():
                to_left(m, j).wait_send()

        @pl.when(section > 0)
        def _():
            hop(m).wait_send()

        g_keep(m).wait()

        @pl.loop(1, replicas)
        def _(o):
            g_share(m, o).wait_send()
            g_share(m, o).wait_recv()

    x_keep().wait()

    @pl.loop(1, replicas)
    def _(o):
        x_share(o).wait_send()
        x_share(o).wait_recv()


def per_device(weights, codes, scales, grad_out):
    sections, shards, replicas = (lax.axis_size(n) for n in ("pipe", "tensor", "dp"))
    tok, cols = grad_out.shape
    depth = weights.shape[1]
    width = depth // replicas
    rows = tok // MICRO
    low = jnp.bfloat16
    dma = pltpu.SemaphoreType.DMA
    anywhere = pl.BlockSpec(memory_space=pl.ANY)
    inside = pl.BlockSpec(memory_space=pltpu.VMEM)
    grad_in, g_all, x_all = pl.pallas_call(
        functools.partial(relay_kernel, sections=sections, shards=shards, replicas=replicas, micro=MICRO),
        out_shape=(
            jax.ShapeDtypeStruct((tok, cols), low),
            jax.ShapeDtypeStruct((replicas * tok, cols), low),
            jax.ShapeDtypeStruct((replicas * tok, width), low),
        ),
        in_specs=[anywhere, anywhere, inside, anywhere],
        out_specs=(inside, anywhere, anywhere),
        scratch_shapes=[
            pltpu.VMEM((depth, cols), low),
            pltpu.VMEM((replicas, tok, width), jnp.int32),
            pltpu.VMEM((replicas, tok, width), low),
            pltpu.VMEM((tok, cols), low),
            pltpu.VMEM((MICRO, shards, rows, cols), low),
            pltpu.VMEM((MICRO, shards, rows, cols), low),
            pltpu.VMEM((MICRO, shards, rows, cols), low),
            dma((shards,)), dma((replicas,)), dma((MICRO,)), dma((MICRO,)),
            dma((MICRO, shards)), dma((MICRO, shards)), dma((MICRO, shards)), dma((MICRO, shards)),
            dma((MICRO, replicas)), dma((MICRO, replicas)), dma((replicas,)), dma((replicas,)),
            dma((MICRO,)), dma(()),
        ],
        compiler_params=pltpu.CompilerParams(collective_id=0, has_side_effects=True, vmem_limit_bytes=48 * 2**20),
    )(weights[0], codes[0], scales[0][:, None], grad_out)
    weight_grad = lax.dot_general(x_all, g_all, (((0,), (0,)), ((), ())), preferred_element_type=jnp.float32)
    return grad_in[None], weight_grad[None]


def solution(mesh):
    placed = (P("pipe", None, "tensor"), P("pipe", "dp", None), P("pipe", "dp"), P("dp", "tensor"))
    return jax.shard_map(
        per_device,
        mesh=mesh,
        in_specs=placed,
        out_specs=(P("pipe", "dp", "tensor"), P("pipe", "dp", "tensor")),
        check_vma=False,
    )
```

time: 225 us -> 72.2 us (0.32)
  waiting for transfers between devices: 141 us -> 0 us
  Pallas kernels: 0 us -> 64.4 us
  matrix products: 40.7 us -> 4.4 us
  between operations: 14.3 us -> 0.65 us
  other arithmetic: 13.6 us -> 0 us
  starting transfers between devices: 9.21 us -> 0 us
  local copies, waits for them, and re-layouts: 5.78 us -> 2.64 us
    reduce_scatter x5 -> x0, waiting for transfers between devices: 83.4 us -> none  [per_device(): lax.psum_scatter(partial_value.astype(jnp.bfloat16), 'tensor', scatter_di...]
    pallas_call x0 -> x1, Pallas kernels: none -> 64.4 us  [per_device(): pl.pallas_call(functools.partial(relay_kernel, sections=sections, shards=...]
    dot_general x6 -> x1, matrix products: 40.7 us -> 4.4 us  [per_device(): lax.dot_general(x_all, g_all, (((0,), (0,)), ((), ())), preferred_element...]
    all_to_all x1 -> x0, waiting for transfers between devices: 35 us -> none  [per_device(): lax.all_to_all(dequant, 'dp', split_axis=1, concat_axis=0, tiled=True)]
    ppermute x4 -> x0, waiting for transfers between devices: 22.1 us -> none  [shifted(): lax.ppermute(value, axis, [(source, source + steps) for source in range(i...]
    convert_element_type x2 -> x0, other arithmetic: 8.52 us -> none  [the longest x1 4.65 us: per_device(): codes[0].astype(jnp.float32) * scales[0][:, None]]
    convert_element_type x1 -> x0, local copies, waits for them, and re-layouts: 5.62 us -> none  [per_device(): codes[0].astype(jnp.float32) * scales[0][:, None]]
    ppermute x4 -> x0, starting transfers between devices: 5.17 us -> none  [shifted(): lax.ppermute(value, axis, [(source, source + steps) for source in range(i...]
  transfers between devices with their start and end apart: 11 -> 0, of which waited for: 10 -> 0; matrix products, arithmetic and copies ran while one was open for 7% -> 0% of each run, Pallas kernels for 0% -> 0%
where the time goes in v1:
time: 72.2 us; the launch traced here: 72.1 us
  Pallas kernels  64.4 us (89%)
  matrix products  4.4 us (6%)
  local copies, waits for them, and re-layouts  2.64 us (4%)
    pallas_call x1, Pallas kernels, per_device(): pl.pallas_call(functools.partial(relay_kernel, sections=sections, shards=...  64.4 us
    dot_general x1, matrix products, per_device(): lax.dot_general(x_all, g_all, (((0,), (0,)), ((), ())), preferred_element...  4.4 us
    unnamed x3, local copies, waits for them, and re-layouts  1.83 us

profile of v1, /device:TPU:0, one launch (start us, length us, event | category | flops | bytes accessed | tf_op | source)
XLA Modules:
  0.0 72.1 jit_solution(12906430412655731996)
XLA Ops:
  0.6 0.8 %copy.6.scales = f32[256,1]{1,0:T(8,128)S(1)} copy(f32[256,1]{0,1:T(1,128)} %bitcast.11) | data formatting | bytes 2048 | tf_op jit(solution)/shard_map/broadcast_in_dim;squeeze | solution.py:316
  1.4 0.0 copy-start
  1.5 1.0 %copy-done = bf16[256,1024]{1,0:T(8,128)(2,1)S(1)} copy-done((bf16[256,1024]{1,0:T(8,128)(2,1)S(1)}, bf16[256,1024]{1,0:T(8,128)(2,1)}, u32[]{:S(2)}) %copy-start) | copy-done | bytes 524312
  2.5 64.4 %shard_map.59 = (bf16[256,1024]{1,0:T(8,128)(2,1)S(1)}, bf16[1024,1024]{1,0:T(8,128)(2,1)S(1)}, bf16[1024,1024]{1,0:T(8,128)(2,1)S(1)}) custom-call(bf16[4096,1024]{1,0:T(8,128)(2,1)} %bitcast.9, s32[256,4096]{1,0:T(8,128)} %bitcast.10, f32[256,1]{1,0:T(8,128)S(1)} %copy.6.scales, bf16[256,1024]{1,0:T(8,128)(2,1)S(1)} %copy-done), custom_call_target="tpu_custom_call" | custom-call | tf_op jit(solution)/shard_map/pallas_call | solution.py:293
  66.9 4.4 %convolution_bitcast_fusion = f32[1,1024,1024]{2,1,0:T(8,128)} fusion(bf16[1024,1024]{1,0:T(8,128)(2,1)S(1)} %get-tuple-element.6, bf16[1024,1024]{1,0:T(8,128)(2,1)S(1)} %get-tuple-element.7), kind=kOutput, calls=%fused_computation | convolution fusion | flops 2147483648 | bytes 8388608 | tf_op jit(solution)/shard_map/dot_general | solution.py:317
  71.3 0.8 %copy.8 = bf16[1,256,1024]{2,1,0:T(8,128)(2,1)} copy(bf16[1,256,1024]{2,1,0:T(8,128)(2,1)S(1)} %bitcast.8) | data formatting | bytes 1048576
Async XLA Ops:
  1.4 1.0 %copy-start = (bf16[256,1024]{1,0:T(8,128)(2,1)S(1)}, bf16[256,1024]{1,0:T(8,128)(2,1)}, u32[]{:S(2)}) copy-start(bf16[256,1024]{1,0:T(8,128)(2,1)} %grad_out.1) | copy-start | bytes 1572868

commit v2 on v1

v2 whole, which is shorter than its diff:
```python
import functools

import jax
import jax.numpy as jnp
from jax import lax
from jax.experimental import pallas as pl
from jax.experimental.pallas import tpu as pltpu
from jax.sharding import PartitionSpec as P

SIXTEENTHS = (4, 4, 4, 4)
STRIPS = 2
NT = (((1,), (1,)), ((), ()))


def relay_kernel(
    weights, codes, scales, grad_out,
    grad_in, g_all, x_all,
    w_buf, c_buf, s_buf, x_buf, g_buf, prod, from_left, from_right,
    w_sem, c_sem, g_sem, g_hop, hop_sem,
    right_send, right_recv, left_send, left_recv,
    g_send, g_recv, x_send, x_recv, g_own, x_own,
    *, sections, shards, replicas, pieces,
):
    section, shard, replica = (lax.axis_index(n) for n in ("pipe", "tensor", "dp"))
    is_last = section == sections - 1
    tok, cols = g_buf.shape
    micro = len(pieces)
    width = x_buf.shape[2]

    barrier = pltpu.get_barrier_semaphore()

    def greet(condition, target):
        @pl.when(condition)
        def _():
            pl.semaphore_signal(barrier, inc=1, device_id=target)

    def w_copy(j):
        part = pl.ds(pl.multiple_of(j * cols, cols), cols)
        return pltpu.make_async_copy(weights.at[part, :], w_buf.at[part, :], w_sem.at[j])

    def c_copy(o):
        peer = lax.rem(replica + o, replicas)
        part = pl.ds(pl.multiple_of(peer * width, width), width)
        return pltpu.make_async_copy(codes.at[:, part], c_buf.at[o], c_sem.at[o])

    def micro_rows(m):
        return pl.ds(*pieces[m])

    def head(ref, m, j):
        return ref.at[m, j, pl.ds(0, pieces[m][1]), :]

    def strip(m, h):
        size = pieces[m][1] // STRIPS
        return pl.ds(h * size, size)

    def strip_rows(m, h):
        size = pieces[m][1] // STRIPS
        return pl.ds(pieces[m][0] + h * size, size)

    def g_load(m):
        return pltpu.make_async_copy(grad_out.at[micro_rows(m), :], g_buf.at[micro_rows(m), :], g_sem.at[m])

    def order(i):
        return jnp.where(2 * shard < shards, shards - 1 - i, i)

    @pl.when(is_last)
    def _():
        for m in range(micro):
            g_load(m).start()

    @pl.loop(0, shards)
    def _(i):
        w_copy(order(i)).start()

    @pl.loop(0, replicas)
    def _(o):
        c_copy(o).start()

    greet(shard > 0, {"tensor": shard - 1})
    greet(shard < shards - 1, {"tensor": shard + 1})
    greet(section > 0, {"pipe": section - 1})
    greet(section < sections - 1, {"pipe": section + 1})

    @pl.loop(1, replicas)
    def _(o):
        pl.semaphore_signal(barrier, inc=1, device_id={"dp": lax.rem(replica + o, replicas)})

    def one(condition):
        return jnp.where(condition, 1, 0)

    pl.semaphore_wait(
        barrier,
        replicas - 1 + one(shard > 0) + one(shard < shards - 1) + one(section > 0) + one(section < sections - 1),
    )

    def hop(m, h):
        return pltpu.make_async_remote_copy(
            src_ref=grad_in.at[strip_rows(m, h), :], dst_ref=g_buf.at[strip_rows(m, h), :],
            send_sem=hop_sem.at[m * STRIPS + h], recv_sem=g_hop.at[m * STRIPS + h], device_id={"pipe": section - 1})

    def to_right(m, j, h):
        return pltpu.make_async_remote_copy(
            src_ref=prod.at[m, j, strip(m, h), :], dst_ref=from_left.at[m, j, strip(m, h), :],
            send_sem=right_send.at[m * STRIPS + h, j], recv_sem=right_recv.at[m * STRIPS + h, j], device_id={"tensor": shard + 1})

    def to_left(m, j, h):
        return pltpu.make_async_remote_copy(
            src_ref=prod.at[m, j, strip(m, h), :], dst_ref=from_right.at[m, j, strip(m, h), :],
            send_sem=left_send.at[m * STRIPS + h, j], recv_sem=left_recv.at[m * STRIPS + h, j], device_id={"tensor": shard - 1})

    def own_rows(source):
        return pl.ds(pl.multiple_of(source * tok, tok), tok)

    def g_share(m, o):
        landing = pl.ds(pl.multiple_of(replica * tok + pieces[m][0], 16), pieces[m][1])
        return pltpu.make_async_remote_copy(
            src_ref=g_buf.at[micro_rows(m), :], dst_ref=g_all.at[landing, :],
            send_sem=g_send.at[m, o], recv_sem=g_recv.at[m, o],
            device_id={"dp": lax.rem(replica + o, replicas)})

    def g_keep(m):
        landing = pl.ds(pl.multiple_of(replica * tok + pieces[m][0], 16), pieces[m][1])
        return pltpu.make_async_copy(g_buf.at[micro_rows(m), :], g_all.at[landing, :], g_own.at[m])

    def x_share(o):
        return pltpu.make_async_remote_copy(
            src_ref=x_buf.at[o], dst_ref=x_all.at[own_rows(replica), :],
            send_sem=x_send.at[o], recv_sem=x_recv.at[o],
            device_id={"dp": lax.rem(replica + o, replicas)})

    def x_keep():
        return pltpu.make_async_copy(x_buf.at[0], x_all.at[own_rows(replica), :], x_own)

    def dequantize():
        s_buf[...] = jnp.transpose(jnp.broadcast_to(scales[...], (128, tok)))

        @pl.loop(0, replicas)
        def _(i):
            o = replicas - 1 - i
            c_copy(o).wait()

            @pl.loop(0, 4)
            def _(m):
                part = pl.ds(pl.multiple_of(m * (tok // 4), tok // 4), tok // 4)
                value = c_buf[o, part, :].astype(jnp.float32) * s_buf[part, 0:1]
                x_buf[o, part, :] = value.astype(jnp.bfloat16)

            @pl.when(o > 0)
            def _():
                x_share(o).start()

        x_keep().start()

    def produce(m):
        @pl.when(is_last)
        def _():
            g_load(m).wait()

        @pl.when(jnp.logical_not(is_last))
        def _():
            for h in range(STRIPS):
                hop(m, h).wait_recv()

        @pl.loop(0, shards)
        def _(i):
            j = order(i)

            if m == 0:
                w_copy(j).wait()

            part = pl.ds(pl.multiple_of(j * cols, cols), cols)
            head(prod, m, j)[...] = lax.dot_general(
                g_buf[micro_rows(m), :], w_buf[part, :], NT, preferred_element_type=jnp.float32
            ).astype(jnp.bfloat16)

            @pl.when((shard == 0) & (j > 0))
            def _():
                for h in range(STRIPS):
                    to_right(m, j, h).start()

            @pl.when((shard == shards - 1) & (j < shards - 1))
            def _():
                for h in range(STRIPS):
                    to_left(m, j, h).start()

        g_keep(m).start()

        @pl.loop(1, replicas)
        def _(o):
            g_share(m, o).start()

    def add_in(m, j, h, arrived):
        part = strip(m, h)
        total = prod[m, j, part, :].astype(jnp.float32) + arrived[m, j, part, :].astype(jnp.float32)
        prod[m, j, part, :] = total.astype(jnp.bfloat16)

    def relay(m, rightward):
        @pl.loop(0, shards - 1)
        def _(i):
            far = shards - 1 - i

            @pl.when(rightward & (shard > 0) & (shard + far < shards))
            def _():
                j = shard + far
                for h in range(STRIPS):
                    to_right(m, j, h).wait_recv()
                    add_in(m, j, h, from_left)
                    to_right(m, j, h).start()

            @pl.when(jnp.logical_not(rightward) & (shard < shards - 1) & (shard - far >= 0))
            def _():
                j = shard - far
                for h in range(STRIPS):
                    to_left(m, j, h).wait_recv()
                    add_in(m, j, h, from_right)
                    to_left(m, j, h).start()

    def finish(m, h):
        part, inner = strip_rows(m, h), strip(m, h)

        @pl.when(shard > 0)
        def _():
            to_right(m, shard, h).wait_recv()

        @pl.when(shard < shards - 1)
        def _():
            to_left(m, shard, h).wait_recv()

        def of(ref):
            return ref[m, shard, inner, :].astype(jnp.float32)

        own = of(prod) + g_buf[part, :].astype(jnp.float32)

        @pl.when((shard > 0) & (shard < shards - 1))
        def _():
            grad_in[part, :] = (own + (of(from_left) + of(from_right))).astype(jnp.bfloat16)

        @pl.when(shard == 0)
        def _():
            grad_in[part, :] = (own + of(from_right)).astype(jnp.bfloat16)

        @pl.when(shard == shards - 1)
        def _():
            grad_in[part, :] = (own + of(from_left)).astype(jnp.bfloat16)

        @pl.when(section > 0)
        def _():
            hop(m, h).start()

    @pl.when(jnp.logical_not(is_last))
    def _():
        dequantize()

    near = 2 * shard < shards
    produce(0)

    @pl.when(is_last)
    def _():
        dequantize()

    for m in range(micro):
        relay(m, near)
        relay(m, jnp.logical_not(near))
        if m + 1 < micro:
            produce(m + 1)
        for h in range(STRIPS):
            finish(m, h)

    for m in range(micro):

        @pl.loop(0, shards)
        def _(j):
            @pl.when((j > shard))
            def _():
                for h in range(STRIPS):
                    to_right(m, j, h).wait_send()

            @pl.when((j < shard))
            def _():
                for h in range(STRIPS):
                    to_left(m, j, h).wait_send()

        @pl.when(section > 0)
        def _():
            for h in range(STRIPS):
                hop(m, h).wait_send()

        g_keep(m).wait()

        @pl.loop(1, replicas)
        def _(o):
            g_share(m, o).wait_send()
            g_share(m, o).wait_recv()

    x_keep().wait()

    @pl.loop(1, replicas)
    def _(o):
        x_share(o).wait_send()
        x_share(o).wait_recv()


def per_device(weights, codes, scales, grad_out):
    sections, shards, replicas = (lax.axis_size(n) for n in ("pipe", "tensor", "dp"))
    tok, cols = grad_out.shape
    depth = weights.shape[1]
    width = depth // replicas
    sizes = [tok * part // 16 for part in SIXTEENTHS]
    pieces = tuple((sum(sizes[:m]), size) for m, size in enumerate(sizes))
    micro, rows = len(sizes), max(sizes)
    strips = micro * STRIPS
    low = jnp.bfloat16
    dma = pltpu.SemaphoreType.DMA
    anywhere = pl.BlockSpec(memory_space=pl.ANY)
    far = pl.BlockSpec(memory_space=pltpu.MemorySpace.HBM)
    inside = pl.BlockSpec(memory_space=pltpu.VMEM)
    grad_in, g_all, x_all = pl.pallas_call(
        functools.partial(relay_kernel, sections=sections, shards=shards, replicas=replicas, pieces=pieces),
        out_shape=(
            jax.ShapeDtypeStruct((tok, cols), low),
            jax.ShapeDtypeStruct((replicas * tok, cols), low),
            jax.ShapeDtypeStruct((replicas * tok, width), low),
        ),
        in_specs=[far, far, inside, far],
        out_specs=(inside, anywhere, anywhere),
        scratch_shapes=[
            pltpu.VMEM((depth, cols), low),
            pltpu.VMEM((replicas, tok, width), jnp.int32),
            pltpu.VMEM((tok, 128), jnp.float32),
            pltpu.VMEM((replicas, tok, width), low),
            pltpu.VMEM((tok, cols), low),
            pltpu.VMEM((micro, shards, rows, cols), low),
            pltpu.VMEM((micro, shards, rows, cols), low),
            pltpu.VMEM((micro, shards, rows, cols), low),
            dma((shards,)), dma((replicas,)), dma((micro,)), dma((strips,)), dma((strips,)),
            dma((strips, shards)), dma((strips, shards)), dma((strips, shards)), dma((strips, shards)),
            dma((micro, replicas)), dma((micro, replicas)), dma((replicas,)), dma((replicas,)),
            dma((micro,)), dma(()),
        ],
        compiler_params=pltpu.CompilerParams(collective_id=0, has_side_effects=True, vmem_limit_bytes=48 * 2**20),
    )(weights[0], codes[0], scales, grad_out)
    weight_grad = lax.dot_general(x_all, g_all, (((0,), (0,)), ((), ())), preferred_element_type=jnp.float32)
    return grad_in[None], weight_grad[None]


def solution(mesh):
    placed = (P("pipe", None, "tensor"), P("pipe", "dp", None), P("pipe", "dp"), P("dp", "tensor"))
    return jax.shard_map(
        per_device,
        mesh=mesh,
        in_specs=placed,
        out_specs=(P("pipe", "dp", "tensor"), P("pipe", "dp", "tensor")),
        check_vma=False,
    )
```

time: 72.2 us -> 70.1 us (0.971)
  Pallas kernels: 64.4 us -> 62.3 us
    pallas_call x1, Pallas kernels: 64.4 us -> 62.3 us  [per_device(): pl.pallas_call(functools.partial(relay_kernel, sections=sections, shards=...]
    another operation x1 -> x0, local copies, waits for them, and re-layouts: 0.81 us -> none  [per_device(): scales[0][:, None]]
    unnamed x3 -> x5, local copies, waits for them, and re-layouts: 1.83 us -> 2.51 us
where the time goes in v2:
time: 70.1 us; the launch traced here: 69.9 us
  Pallas kernels  62.3 us (89%)
  matrix products  4.45 us (6%)
  local copies, waits for them, and re-layouts  2.51 us (4%)
    pallas_call x1, Pallas kernels, per_device(): pl.pallas_call(functools.partial(relay_kernel, sections=sections, shards=...  62.3 us
    dot_general x1, matrix products, per_device(): lax.dot_general(x_all, g_all, (((0,), (0,)), ((), ())), preferred_element...  4.45 us
    unnamed x5, local copies, waits for them, and re-layouts  2.51 us

profile of v2, /device:TPU:0, one launch (start us, length us, event | category | flops | bytes accessed | tf_op | source)
XLA Modules:
  0.0 69.9 jit_solution(11780648360539416426)
XLA Ops:
  0.6 0.0 copy-start
  0.6 1.0 %copy-done = bf16[256,1024]{1,0:T(8,128)(2,1)S(1)} copy-done((bf16[256,1024]{1,0:T(8,128)(2,1)S(1)}, bf16[256,1024]{1,0:T(8,128)(2,1)}, u32[]{:S(2)}) %copy-start) | copy-done | bytes 524312
  1.7 0.0 copy-start.1
  1.7 0.7 copy-done.1
  2.4 62.3 %shard_map.59 = (bf16[256,1024]{1,0:T(8,128)(2,1)S(1)}, bf16[1024,1024]{1,0:T(8,128)(2,1)S(1)}, bf16[1024,1024]{1,0:T(8,128)(2,1)S(1)}) custom-call(bf16[4096,1024]{1,0:T(8,128)(2,1)} %bitcast.8, s32[256,4096]{1,0:T(8,128)} %bitcast.9, f32[1,256]{1,0:T(1,128)S(1)} %copy-done.1, bf16[256,1024]{1,0:T(8,128)(2,1)S(1)} %copy-done), custom_call_target="tpu_custom_call" | custom-call | tf_op jit(solution)/shard_map/pallas_call | solution.py:317
  64.7 4.4 %convolution_bitcast_fusion = f32[1,1024,1024]{2,1,0:T(8,128)} fusion(bf16[1024,1024]{1,0:T(8,128)(2,1)S(1)} %get-tuple-element.6, bf16[1024,1024]{1,0:T(8,128)(2,1)S(1)} %get-tuple-element.7), kind=kOutput, calls=%fused_computation | convolution fusion | flops 2147483648 | bytes 8388608 | tf_op jit(solution)/shard_map/dot_general | solution.py:342
  69.1 0.8 %copy.7 = bf16[1,256,1024]{2,1,0:T(8,128)(2,1)} copy(bf16[1,256,1024]{2,1,0:T(8,128)(2,1)S(1)} %bitcast.7) | data formatting | bytes 1048576
Async XLA Ops:
  0.6 1.0 %copy-start = (bf16[256,1024]{1,0:T(8,128)(2,1)S(1)}, bf16[256,1024]{1,0:T(8,128)(2,1)}, u32[]{:S(2)}) copy-start(bf16[256,1024]{1,0:T(8,128)(2,1)} %grad_out.1) | copy-start | bytes 1572868
  1.7 0.7 copy-start.1
